TPU v7x, 32 devices: a whole 2x2x4 slice. The times are simulated.
32 devices in a mesh: groups: 2 (over y), rows: 4 (over z), cols: 4 (over x, core).
Axes of the slice: x: 2, y: 2, z: 4, core: 2. Of those that a mesh axis runs over, the one named last changes fastest.
Arguments:
- hidden: bfloat16 [64, 32, 1280], P(('groups', 'rows'), 'cols'), parts along dimension 0, may hold values from -6 to 6
- ln_gain: float32 [1280], replicated, may hold values from 0.1 to 1.9
- ln_bias: float32 [1280], replicated, may hold values from -3 to 3
- w_query: bfloat16 [1280, 256], P(None, 'cols'), may hold values from -8.944272 to 8.944272
- w_keyval: bfloat16 [1280, 512], P(None, 'cols'), may hold values from -0.3125 to 0.3125
- stale_keyval: bfloat16 [64, 32, 4, 128], P(('groups', 'rows'), None, 'cols'), parts along dimension 0, may hold values from -10 to 10
- w_out: bfloat16 [256, 1280], replicated, may hold values from -0.375 to 0.375
- out_bias: float32 [1280], replicated, may hold values from -3 to 3
Outputs:
- output_rows: bfloat16 [64, 32, 1280], P(('groups', 'rows'), 'cols'), parts along dimension 0
- fresh_keyval: bfloat16 [64, 32, 4, 128], P(('groups', 'rows'), None, 'cols'), parts along dimension 0
There are 2 independent parts, one for each index of `groups`. A program takes and returns all parts, laid end to end along the dimension named above; an argument that names none is the same for every part. Nothing has to cross between parts.
All inputs are finite; a program needn't handle non-finite values.
Results may differ from a plain program's by a relative error of at most 0.04.
The roundings to bfloat16 on the way count: a program that leaves them out, or rounds other values in their place, can miss the bound.
Values may be sent and summed in bfloat16 or wider, within the bound.
No kernel may reach another device: no remote copies, remote signals or barrier semaphores. Data moves between devices by JAX's collectives and lax.ppermute only.
A program may use at most 64 MiB of HBM per device.

v0:
```python
import math
import jax
import jax.numpy as jnp
from jax import lax
from jax.sharding import PartitionSpec as P


def layer_norm(hidden, ln_gain, ln_bias):
    values = hidden.astype(jnp.float32)
    row_mean = jnp.mean(values, axis=-1, keepdims=True)
    centred = values - row_mean
    variance = jnp.mean(centred * centred, axis=-1, keepdims=True)
    return (centred * lax.rsqrt(variance + 1e-05) * ln_gain + ln_bias).astype(jnp.bfloat16)


def absorb(running, key_block, queries, score_scale):
    row_max, denominator, weighted = running
    head_size = queries.shape[1]
    scores = (
        jnp.dot(queries, key_block[:, :head_size].T, preferred_element_type=jnp.float32)
        * score_scale
    )
    new_max = jnp.maximum(row_max, jnp.max(scores, axis=-1))
    factor = jnp.exp(row_max - new_max)
    probability = jnp.exp(scores - new_max[:, None])
    denominator = denominator * factor + jnp.sum(probability, axis=-1)
    weighted = weighted * factor[:, None] + jnp.dot(
        probability.astype(jnp.bfloat16),
        key_block[:, head_size:],
        preferred_element_type=jnp.float32,
    )
    return (new_max, denominator, weighted)


def shards(hidden, ln_gain, ln_bias, w_query, w_keyval, stale_keyval, w_out, out_bias):
    band_rows, strip_cols, channels = hidden.shape
    head_size = w_query.shape[1]
    normed = layer_norm(hidden, ln_gain, ln_bias)
    both_weights = jnp.concatenate([w_query, w_keyval], axis=1)
    projected = jnp.dot(
        lax.all_gather(normed, "cols", axis=1, tiled=True),
        both_weights,
        preferred_element_type=jnp.float32,
    ).astype(jnp.bfloat16)
    full_cols = projected.shape[1]
    queries = projected[:, :, :head_size].reshape(-1, head_size)
    keyval = projected[:, :, head_size:]
    fresh_flat = keyval.reshape(-1, 2 * head_size)
    own_band = lax.axis_index("rows")
    score_scale = 1.0 / math.sqrt(head_size)
    query_count = queries.shape[0]
    initial = (
        jnp.full((query_count,), -1e30, jnp.float32),
        jnp.zeros((query_count,), jnp.float32),
        jnp.zeros((query_count, head_size), jnp.float32),
    )
    received = lax.all_gather(stale_keyval, "rows", axis=0, tiled=True)
    band_count = received.shape[0] // band_rows
    key_blocks = received.reshape(band_count, band_rows * full_cols, 2 * head_size)

    def step_band(state, position):
        key_block = jnp.where(position == own_band, fresh_flat, key_blocks[position])
        return (absorb(state, key_block, queries, score_scale), None)

    folded, unused = lax.scan(step_band, initial, jnp.arange(band_count, dtype=jnp.int32))
    row_max, denominator, weighted = folded
    attention = (
        (weighted / denominator[:, None])
        .astype(jnp.bfloat16)
        .reshape(band_rows, full_cols, 1, head_size)
    )
    values = lax.all_to_all(attention, "cols", split_axis=1, concat_axis=2, tiled=True)
    row_count = values.shape[0]
    flat_values = values.reshape(row_count * values.shape[1], values.shape[2] * values.shape[3])
    result = jnp.dot(flat_values, w_out, preferred_element_type=jnp.float32)
    projected_out = result.reshape(row_count, values.shape[1], channels)
    output_rows = (projected_out + out_bias + hidden.astype(jnp.float32)).astype(jnp.bfloat16)
    return (output_rows, keyval.reshape(band_rows, full_cols, 1, 2 * head_size))


def solution(mesh):
    return jax.shard_map(
        shards,
        mesh=mesh,
        in_specs=(
            P(("groups", "rows"), "cols", None),
            P(),
            P(),
            P(None, "cols"),
            P(None, "cols"),
            P(("groups", "rows"), None, "cols", None),
            P(),
            P(),
        ),
        out_specs=(P(("groups", "rows"), "cols", None), P(("groups", "rows"), None, "cols", None)),
        check_vma=False,
    )
```

profile of v0, /device:TPU:0, one launch (start us, length us, event | category | flops | bytes accessed | tf_op | source)
XLA Modules:
  0.0 53.3 jit_solution(13207126210081687228)
XLA Ops:
  0.6 0.0 copy-start
  0.6 0.0 copy-start.1
  0.7 1.1 %convert_reduce_fusion = f32[8,8]{1,0:T(8,128)S(1)} fusion(bf16[8,8,1280]{2,1,0:T(8,128)(2,1)} %param.10), kind=kLoop, calls=%fused_computation.24 | loop fusion | flops 163776 | bytes 164096 | tf_op jit(solution)/shard_map/reduce_sum | solution.py:10
  1.8 0.0 copy-done.1
  1.8 0.0 copy-start.7
  1.8 0.2 fusion.15
  2.0 0.5 copy-done.7
  2.5 0.2 copy-done.6
  2.7 0.1 fusion.18
  2.8 0.0 copy-start.3
  2.8 9.5 %all_gather.7 = bf16[8,32,1280]{2,1,0:T(8,128)(2,1)S(1)} all-gather(bf16[8,8,1280]{2,1,0:T(8,128)(2,1)S(1)} %fusion.18), channel_id=1, replica_groups=mesh['groups'=2,'rows'=4,'cols'=4] {'cols'}, dimensions={1}, use_global_device_ids=true | all-gather | bytes 819200 | tf_op jit(solution)/shard_map/all_gather | solution.py:41
  12.3 0.0 copy-done.3
  12.3 0.2 copy.16
  12.5 0.7 %copy-done.8 = bf16[1280,64]{0,1:T(8,128)(2,1)S(1)} copy-done((bf16[1280,64]{0,1:T(8,128)(2,1)S(1)}, bf16[1280,64]{0,1:T(8,128)(2,1)}, u32[]{:S(2)}) %copy-start.8) | copy-done | bytes 163864
  13.2 0.3 convolution_convert_fusion
  13.6 0.0 copy-start.2
  13.6 0.7 %slice_bitcast_fusion = (bf16[8,32,1,128]{3,1,2,0:T(8,128)(2,1)}, bf16[8,32,128]{2,1,0:T(8,128)(2,1)S(1)}) fusion(bf16[8,32,192]{2,1,0:T(8,128)(2,1)S(1)} %convolution_convert_fusion), kind=kLoop, calls=%fused_computation.36 | loop fusion | bytes 196608
  14.3 0.0 copy-done.2
  14.3 0.8 %copy-done.4 = bf16[8,32,1,128]{3,1,2,0:T(8,128)(2,1)S(1)} copy-done((bf16[8,32,1,128]{3,1,2,0:T(8,128)(2,1)S(1)}, bf16[8,32,1,128]{3,1,2,0:T(8,128)(2,1)}, u32[]{:S(2)}) %copy-start.4) | copy-done | bytes 65560
  15.2 14.3 %all_gather.6 = bf16[32,32,1,128]{3,1,2,0:T(8,128)(2,1)S(1)} all-gather(bf16[8,32,1,128]{3,1,2,0:T(8,128)(2,1)S(1)} %copy-done.4), channel_id=1, replica_groups=mesh['groups'=2,'rows'=4,'cols'=4] {'rows'}, dimensions={0}, use_global_device_ids=true | all-gather | bytes 327680 | tf_op jit(solution)/shard_map/all_gather | solution.py:57
  29.5 0.0 slice-done
  29.5 15.4 %while.15 = (s32[]{:T(128)}, f32[256]{0:T(256)S(1)}, f32[256]{0:T(256)S(1)}, f32[256,64]{0,1:T(8,128)S(1)}, s32[4]{0:T(128)S(1)}, /*index=5*/s32[]{:T(128)}, bf1...) while((s32[]{:T(128)}, f32[256]{0:T(256)S(1)}, ...), condition=%wide.region_5.6_spmd.clone, body=%wide.region_2.5_spmd.clone.sunk | while | flops 17253640 | bytes 1294525 | solution.py:65
  29.5 0.6 %dynamic_slice.13 = s32[1]{0:T(128)} dynamic-slice(s32[4]{0:T(128)S(1)} %get-tuple-element.203, s32[]{:T(128)} %get-tuple-element.187), dynamic_slice_sizes={1} | dynamic-slice | bytes 12 | tf_op jit(solution)/shard_map/while/body/jit(dynamic_index_in_dim)/dynamic_slice | solution.py:65
  32.7 0.2 fusion.34
  32.9 0.1 fusion.36
  33.0 0.3 convolution_add_fusion.3
  33.3 0.6 %dynamic_slice.13 = s32[1]{0:T(128)} dynamic-slice(s32[4]{0:T(128)S(1)} %get-tuple-element.203, s32[]{:T(128)} %get-tuple-element.187), dynamic_slice_sizes={1} | dynamic-slice | bytes 12 | tf_op jit(solution)/shard_map/while/body/jit(dynamic_index_in_dim)/dynamic_slice | solution.py:65
  36.5 0.2 fusion.34
  36.8 0.1 fusion.36
  36.9 0.3 convolution_add_fusion.3
  37.2 0.6 %dynamic_slice.13 = s32[1]{0:T(128)} dynamic-slice(s32[4]{0:T(128)S(1)} %get-tuple-element.203, s32[]{:T(128)} %get-tuple-element.187), dynamic_slice_sizes={1} | dynamic-slice | bytes 12 | tf_op jit(solution)/shard_map/while/body/jit(dynamic_index_in_dim)/dynamic_slice | solution.py:65
  40.4 0.2 fusion.34
  40.6 0.1 fusion.36
  40.7 0.3 convolution_add_fusion.3
  41.0 0.6 %dynamic_slice.13 = s32[1]{0:T(128)} dynamic-slice(s32[4]{0:T(128)S(1)} %get-tuple-element.203, s32[]{:T(128)} %get-tuple-element.187), dynamic_slice_sizes={1} | dynamic-slice | bytes 12 | tf_op jit(solution)/shard_map/while/body/jit(dynamic_index_in_dim)/dynamic_slice | solution.py:65
  44.2 0.2 fusion.34
  44.5 0.1 fusion.36
  44.6 0.3 convolution_add_fusion.3
  44.9 0.1 copy.17
  45.0 0.1 divide_convert_fusion
  45.1 0.1 reshape.49
  45.2 6.3 %all_to_all.15 = bf16[4,2,2048]{2,1,0:T(2,128)(2,1)S(1)} all-to-all(bf16[4,2,2048]{2,1,0:T(2,128)(2,1)S(1)} %reshape.49), channel_id=1, replica_groups=mesh['groups'=2,'rows'=4,'cols'=4] {'cols'}, dimensions={0} | all-to-all | bytes 65536 | tf_op jit(solution)/shard_map/all_to_all | solution.py:72
  51.5 0.1 reshape.50
  51.7 0.0 copy-start.5
  51.7 0.1 dot_general.15
  51.8 0.0 copy-done
  51.8 0.6 %copy-done.5 = f32[1280]{0:T(1024)S(1)} copy-done((f32[1280]{0:T(1024)S(1)}, f32[1280]{0:T(1024)}, u32[]{:S(2)}) %copy-start.5) | copy-done | bytes 5144
  52.4 0.9 %fusion.9 = bf16[8,8,1280]{2,1,0:T(8,128)(2,1)} fusion(bf16[8,8,256]{2,1,0:T(8,128)(2,1)S(1)} %dot_general.15, bf16[256,1280]{1,0:T(8,128)(2,1)S(1)} %copy-done, bf16[8,8,1280]{2,1,0:T(8,128)(2,1)S(1)} %copy-done.1, f32[1280]{0:T(1024)S(1)} %copy-done.5), kind=kOutput, calls=%fused_computation.17 | convolution fusion | flops 42270720 | bytes 1020928 | tf_op jit(solution)/shard_map/dot_general | solution.py:75
  (29 shorter events, 0.2 us)
Async XLA Ops:
  0.6 51.2 %copy-start = (bf16[256,1280]{1,0:T(8,128)(2,1)S(1)}, bf16[256,1280]{1,0:T(8,128)(2,1)}, u32[]{:S(2)}) copy-start(bf16[256,1280]{1,0:T(8,128)(2,1)} %param.16) | copy-start | bytes 1966084
  0.6 1.1 %copy-start.1 = (bf16[8,8,1280]{2,1,0:T(8,128)(2,1)S(1)}, bf16[8,8,1280]{2,1,0:T(8,128)(2,1)}, u32[]{:S(2)}) copy-start(bf16[8,8,1280]{2,1,0:T(8,128)(2,1)} %param.10) | copy-start | bytes 491524
  1.8 0.7 %copy-start.7 = (f32[1280]{0:T(1024)S(1)}, f32[1280]{0:T(1024)}, u32[]{:S(2)}) copy-start(f32[1280]{0:T(1024)} %param.11) | copy-start | bytes 15364
  2.0 0.7 %copy-start.6 = (f32[1280]{0:T(1024)S(1)}, f32[1280]{0:T(1024)}, u32[]{:S(2)}) copy-start(f32[1280]{0:T(1024)} %param.12) | copy-start | bytes 15364
  2.8 9.5 %copy-start.3 = (bf16[1280,128]{1,0:T(8,128)(2,1)S(1)}, bf16[1280,128]{1,0:T(8,128)(2,1)}, u32[]{:S(2)}) copy-start(bf16[1280,128]{1,0:T(8,128)(2,1)} %param.14) | copy-start | bytes 983044
  12.3 0.9 %copy-start.8 = (bf16[1280,64]{0,1:T(8,128)(2,1)S(1)}, bf16[1280,64]{0,1:T(8,128)(2,1)}, u32[]{:S(2)}) copy-start(bf16[1280,64]{0,1:T(8,128)(2,1)} %param.13) | copy-start | bytes 491524
  13.6 0.7 %copy-start.2 = (bf16[8,32,192]{2,1,0:T(8,128)(2,1)}, bf16[8,32,192]{2,1,0:T(8,128)(2,1)S(1)}, u32[]{:S(2)}) copy-start(bf16[8,32,192]{2,1,0:T(8,128)(2,1)S(1)} %convolution_convert_fusion) | copy-start | bytes 294916
  14.3 0.8 %copy-start.4 = (bf16[8,32,1,128]{3,1,2,0:T(8,128)(2,1)S(1)}, bf16[8,32,1,128]{3,1,2,0:T(8,128)(2,1)}, u32[]{:S(2)}) copy-start(bf16[8,32,1,128]{3,1,2,0:T(8,128)(2,1)} %param.15) | copy-start | bytes 196612
  15.2 14.3 %slice-start = ((bf16[8,32,192]{2,1,0:T(8,128)(2,1)}), bf16[8,32,64]{2,1,0:T(8,128)(2,1)S(1)}, s32[]{:S(2)}) async-start(bf16[8,32,192]{2,1,0:T(8,128)(2,1)} %copy-done.2), calls=%async_computation.1 | async-start | bytes 131072 | tf_op jit(solution)/shard_map/slice | solution.py:46
  51.7 0.7 %copy-start.5 = (f32[1280]{0:T(1024)S(1)}, f32[1280]{0:T(1024)}, u32[]{:S(2)}) copy-start(f32[1280]{0:T(1024)} %param.17) | copy-start | bytes 15364
where the time goes:
time: 53.9 us; the launch traced here: 53.3 us
  blocking collectives  30.1 us (56%)
  loops' own time  10.6 us (20%)
  local copies, waits for them, and re-layouts  6.62 us (12%)
  matrix products  3.3 us (6%)
  other arithmetic  1.97 us (4%)
  between operations  0.77 us (1%)
    all_gather x1, blocking collectives, shards(): received = lax.all_gather(stale_keyval, 'rows', axis=0, tiled=True)  14.3 us
    another operation x1, loops' own time, shards(): lax.scan(step_band, initial, jnp.arange(band_count, dtype=jnp.int32))  10.6 us
    all_gather x1, blocking collectives, shards(): lax.all_gather(normed, 'cols', axis=1, tiled=True)  9.49 us
    all_to_all x1, blocking collectives, shards(): lax.all_to_all(attention, 'cols', split_axis=1, concat_axis=2, tiled=True)  6.3 us
    unnamed x22, local copies, waits for them, and re-layouts  3.99 us
    dynamic_slice x4, local copies, waits for them, and re-layouts, shards(): lax.scan(step_band, initial, jnp.arange(band_count, dtype=jnp.int32))  2.34 us
    dot_general x4, matrix products, absorb(): jnp.dot(probability.astype(jnp.bfloat16), key_block[:, head_size:], prefe...  1.16 us
    reduce_sum x1, other arithmetic, layer_norm(): row_mean = jnp.mean(values, axis=-1, keepdims=True)  1.1 us

commit v1 on v0

--- a/solution.py
+++ b/solution.py
@@ -69,7 +69,15 @@
         .astype(jnp.bfloat16)
         .reshape(band_rows, full_cols, 1, head_size)
     )
-    values = lax.all_to_all(attention, "cols", split_axis=1, concat_axis=2, tiled=True)
+    ways, here = (lax.axis_size("cols"), lax.axis_index("cols"))
+    width = attention.shape[1] // ways
+    turned = jnp.roll(attention, -here * width, axis=1)
+    got = [lax.slice_in_dim(turned, 0, width, axis=1)]
+    for far in range(1, ways):
+        sent = lax.slice_in_dim(turned, far * width, (far + 1) * width, axis=1)
+        got.append(lax.ppermute(sent, "cols", [(d, (d + far) % ways) for d in range(ways)]))
+    line = jnp.concatenate(got[::-1], axis=2)
+    values = jnp.roll(line, (here + 1) * got[0].shape[2], axis=2)
     row_count = values.shape[0]
     flat_values = values.reshape(row_count * values.shape[1], values.shape[2] * values.shape[3])
     result = jnp.dot(flat_values, w_out, preferred_element_type=jnp.float32)

time: 53.9 us -> 51.8 us (0.961)
  blocking collectives: 30.1 us -> 23.7 us
  waiting for transfers between devices: 0 us -> 3 us
  starting transfers between devices: 0 us -> 1.36 us
    all_to_all x1 -> x0, blocking collectives: 6.3 us -> none  [shards(): lax.all_to_all(attention, 'cols', split_axis=1, concat_axis=2, tiled=True)]
    ppermute x0 -> x3, waiting for transfers between devices: none -> 3 us  [shards(): lax.ppermute(sent, 'cols', [(d, (d + far) % ways) for d in range(ways)])]
    ppermute x0 -> x3, starting transfers between devices: none -> 1.36 us  [shards(): lax.ppermute(sent, 'cols', [(d, (d + far) % ways) for d in range(ways)])]
    unnamed x22 -> x27, local copies, waits for them, and re-layouts: 3.99 us -> 3.82 us
  transfers between devices with their start and end apart: 0 -> 3, of which waited for: 0 -> 3; matrix products, arithmetic and copies ran while one was open for 0% -> 0% of each run, Pallas kernels for 0% -> 0%
where the time goes in v1:
time: 51.8 us; the launch traced here: 51.3 us
  blocking collectives  23.7 us (46%)
  loops' own time  10.6 us (20%)
  local copies, waits for them, and re-layouts  6.47 us (12%)
  matrix products  3.29 us (6%)
  waiting for transfers between devices  3 us (6%)
  other arithmetic  2.05 us (4%)
  starting transfers between devices  1.36 us (3%)
  between operations  0.82 us (2%)
    all_gather x1, blocking collectives, shards(): received = lax.all_gather(stale_keyval, 'rows', axis=0, tiled=True)  14.2 us
    another operation x1, loops' own time, shards(): lax.scan(step_band, initial, jnp.arange(band_count, dtype=jnp.int32))  10.6 us
    all_gather x1, blocking collectives, shards(): lax.all_gather(normed, 'cols', axis=1, tiled=True)  9.49 us
    unnamed x27, local copies, waits for them, and re-layouts  3.82 us
    ppermute x3, waiting for transfers between devices, shards(): lax.ppermute(sent, 'cols', [(d, (d + far) % ways) for d in range(ways)])  3 us
    dynamic_slice x4, local copies, waits for them, and re-layouts, shards(): lax.scan(step_band, initial, jnp.arange(band_count, dtype=jnp.int32))  2.34 us
    ppermute x3, starting transfers between devices, shards(): lax.ppermute(sent, 'cols', [(d, (d + far) % ways) for d in range(ways)])  1.36 us
    dot_general x4, matrix products, absorb(): jnp.dot(probability.astype(jnp.bfloat16), key_block[:, head_size:], prefe...  1.16 us
  transfers between devices with their start and end apart: 3, of which 3 were waited for; matrix products, arithmetic and copies ran while one was open for 0% of the time, Pallas kernels for 0%

profile of v1, /device:TPU:0, one launch (start us, length us, event | category | flops | bytes accessed | tf_op | source)
XLA Modules:
  0.0 51.3 jit_solution(16025588693416389132)
XLA Ops:
  0.6 0.0 copy-start
  0.7 1.1 %convert_reduce_fusion = f32[8,8]{1,0:T(8,128)S(1)} fusion(bf16[8,8,1280]{2,1,0:T(8,128)(2,1)} %param.10), kind=kLoop, calls=%fused_computation.24 | loop fusion | flops 163776 | bytes 164096 | tf_op jit(solution)/shard_map/reduce_sum | solution.py:10
  1.8 0.0 copy-done.1
  1.8 0.0 copy-start.7
  1.8 0.2 fusion.15
  2.0 0.5 copy-done.7
  2.5 0.2 copy-done.6
  2.7 0.1 fusion.18
  2.9 0.0 copy-start.3
  2.9 9.5 %all_gather.7 = bf16[8,32,1280]{2,1,0:T(8,128)(2,1)S(1)} all-gather(bf16[8,8,1280]{2,1,0:T(8,128)(2,1)S(1)} %fusion.18), channel_id=1, replica_groups=mesh['groups'=2,'rows'=4,'cols'=4] {'cols'}, dimensions={1}, use_global_device_ids=true | all-gather | bytes 819200 | tf_op jit(solution)/shard_map/all_gather | solution.py:41
  12.4 0.2 copy.18
  12.5 0.7 %copy-done.8 = bf16[1280,64]{0,1:T(8,128)(2,1)S(1)} copy-done((bf16[1280,64]{0,1:T(8,128)(2,1)S(1)}, bf16[1280,64]{0,1:T(8,128)(2,1)}, u32[]{:S(2)}) %copy-start.8) | copy-done | bytes 163864
  13.3 0.3 convolution_convert_fusion
  13.6 0.0 copy-start.2
  13.6 0.7 %slice_bitcast_fusion = (bf16[8,32,1,128]{3,1,2,0:T(8,128)(2,1)}, bf16[8,32,128]{2,1,0:T(8,128)(2,1)S(1)}) fusion(bf16[8,32,192]{2,1,0:T(8,128)(2,1)S(1)} %convolution_convert_fusion), kind=kLoop, calls=%fused_computation.47 | loop fusion | bytes 196608
  14.4 0.8 %copy-done.4 = bf16[8,32,1,128]{3,1,2,0:T(8,128)(2,1)S(1)} copy-done((bf16[8,32,1,128]{3,1,2,0:T(8,128)(2,1)S(1)}, bf16[8,32,1,128]{3,1,2,0:T(8,128)(2,1)}, u32[]{:S(2)}) %copy-start.4) | copy-done | bytes 65560
  15.2 14.2 %all_gather.6 = bf16[32,32,1,128]{3,1,2,0:T(8,128)(2,1)S(1)} all-gather(bf16[8,32,1,128]{3,1,2,0:T(8,128)(2,1)S(1)} %copy-done.4), channel_id=1, replica_groups=mesh['groups'=2,'rows'=4,'cols'=4] {'rows'}, dimensions={0}, use_global_device_ids=true | all-gather | bytes 327680 | tf_op jit(solution)/shard_map/all_gather | solution.py:57
  29.4 15.4 %while.15 = (s32[]{:T(128)}, f32[256]{0:T(256)S(1)}, f32[256]{0:T(256)S(1)}, f32[256,64]{0,1:T(8,128)S(1)}, s32[4]{0:T(128)S(1)}, /*index=5*/s32[]{:T(128)}, bf1...) while((s32[]{:T(128)}, f32[256]{0:T(256)S(1)}, ...), condition=%wide.region_5.6_spmd.clone, body=%wide.region_2.5_spmd.clone.sunk | while | flops 17253640 | bytes 1294525 | solution.py:65
  29.4 0.6 %dynamic_slice.32 = s32[1]{0:T(128)} dynamic-slice(s32[4]{0:T(128)S(1)} %get-tuple-element.206, s32[]{:T(128)} %get-tuple-element.190), dynamic_slice_sizes={1} | dynamic-slice | bytes 12 | tf_op jit(solution)/shard_map/while/body/jit(dynamic_index_in_dim)/dynamic_slice | solution.py:65
  32.6 0.2 fusion.36
  32.9 0.1 fusion.38
  32.9 0.3 convolution_add_fusion.3
  33.3 0.6 %dynamic_slice.32 = s32[1]{0:T(128)} dynamic-slice(s32[4]{0:T(128)S(1)} %get-tuple-element.206, s32[]{:T(128)} %get-tuple-element.190), dynamic_slice_sizes={1} | dynamic-slice | bytes 12 | tf_op jit(solution)/shard_map/while/body/jit(dynamic_index_in_dim)/dynamic_slice | solution.py:65
  36.5 0.2 fusion.36
  36.7 0.1 fusion.38
  36.8 0.3 convolution_add_fusion.3
  37.1 0.6 %dynamic_slice.32 = s32[1]{0:T(128)} dynamic-slice(s32[4]{0:T(128)S(1)} %get-tuple-element.206, s32[]{:T(128)} %get-tuple-element.190), dynamic_slice_sizes={1} | dynamic-slice | bytes 12 | tf_op jit(solution)/shard_map/while/body/jit(dynamic_index_in_dim)/dynamic_slice | solution.py:65
  40.3 0.2 fusion.36
  40.6 0.1 fusion.38
  40.6 0.3 convolution_add_fusion.3
  41.0 0.6 %dynamic_slice.32 = s32[1]{0:T(128)} dynamic-slice(s32[4]{0:T(128)S(1)} %get-tuple-element.206, s32[]{:T(128)} %get-tuple-element.190), dynamic_slice_sizes={1} | dynamic-slice | bytes 12 | tf_op jit(solution)/shard_map/while/body/jit(dynamic_index_in_dim)/dynamic_slice | solution.py:65
  44.2 0.2 fusion.36
  44.4 0.1 fusion.38
  44.5 0.3 convolution_add_fusion.3
  44.8 0.1 copy.19
  44.9 0.1 divide_convert_fusion
  45.0 0.1 fusion.19
  45.1 0.1 collective-permute-start
  45.2 1.2 %collective-permute-start.1 = (bf16[8,8,1,64]{3,1,0,2:T(8,128)(2,1)S(1)}, bf16[8,8,1,64]{3,1,0,2:T(8,128)(2,1)S(1)}, u32[]{:S(2)}, u32[]{:S(2)}) collective-permute-start(bf16[8,8,1,64]{3,1,0,2:T(8,128)(2,1)S(1)} %get-tuple-element.113), channel_id=1, source_target_pairs={{0,2},{1,3},{2,0},{3,1},{4,6},{5,7},{6,4},{7,5},{8,10},{9,11},{10,... | collective-permute-start | bytes 24584 | tf_op jit(solution)/shard_map/ppermute | solution.py:78
  46.3 0.2 collective-permute-start.2
  46.5 0.1 collective-permute-done
  46.6 2.4 %collective-permute-done.1 = bf16[8,8,1,64]{3,1,0,2:T(8,128)(2,1)S(1)} collective-permute-done((bf16[8,8,1,64]{3,1,0,2:T(8,128)(2,1)S(1)}, bf16[8,8,1,64]{3,1,0,2:T(8,128)(2,1)S(1)}, u32[]{:S(2)}, u32[]{:S(2)}) %collective-permute-start.1) | collective-permute-done | bytes 8224 | tf_op jit(solution)/shard_map/ppermute | solution.py:78
  49.0 0.5 collective-permute-done.2
  49.6 0.1 copy.20
  49.6 0.0 copy-start.5
  49.7 0.1 dot_general.15
  49.8 0.6 %copy-done.5 = f32[1280]{0:T(1024)S(1)} copy-done((f32[1280]{0:T(1024)S(1)}, f32[1280]{0:T(1024)}, u32[]{:S(2)}) %copy-start.5) | copy-done | bytes 5144
  50.3 0.9 %fusion.9 = bf16[8,8,1280]{2,1,0:T(8,128)(2,1)} fusion(bf16[8,8,256]{2,1,0:T(8,128)(2,1)S(1)} %dot_general.15, bf16[256,1280]{1,0:T(8,128)(2,1)S(1)} %copy-done, bf16[8,8,1280]{2,1,0:T(8,128)(2,1)S(1)} %copy-done.1, f32[1280]{0:T(1024)S(1)} %copy-done.5), kind=kOutput, calls=%fused_computation.17 | convolution fusion | flops 42270720 | bytes 1020928 | tf_op jit(solution)/shard_map/dot_general | solution.py:83
  (41 shorter events, 0.3 us)
Async XLA Ops:
  0.6 49.1 %copy-start = (bf16[256,1280]{1,0:T(8,128)(2,1)S(1)}, bf16[256,1280]{1,0:T(8,128)(2,1)}, u32[]{:S(2)}) copy-start(bf16[256,1280]{1,0:T(8,128)(2,1)} %param.16) | copy-start | bytes 1966084
  0.6 1.2 %copy-start.1 = (bf16[8,8,1280]{2,1,0:T(8,128)(2,1)S(1)}, bf16[8,8,1280]{2,1,0:T(8,128)(2,1)}, u32[]{:S(2)}) copy-start(bf16[8,8,1280]{2,1,0:T(8,128)(2,1)} %param.10) | copy-start | bytes 491524
  1.8 0.7 %copy-start.7 = (f32[1280]{0:T(1024)S(1)}, f32[1280]{0:T(1024)}, u32[]{:S(2)}) copy-start(f32[1280]{0:T(1024)} %param.11) | copy-start | bytes 15364
  2.0 0.7 %copy-start.6 = (f32[1280]{0:T(1024)S(1)}, f32[1280]{0:T(1024)}, u32[]{:S(2)}) copy-start(f32[1280]{0:T(1024)} %param.12) | copy-start | bytes 15364
  2.9 9.5 %copy-start.3 = (bf16[1280,128]{1,0:T(8,128)(2,1)S(1)}, bf16[1280,128]{1,0:T(8,128)(2,1)}, u32[]{:S(2)}) copy-start(bf16[1280,128]{1,0:T(8,128)(2,1)} %param.14) | copy-start | bytes 983044
  12.4 0.9 %copy-start.8 = (bf16[1280,64]{0,1:T(8,128)(2,1)S(1)}, bf16[1280,64]{0,1:T(8,128)(2,1)}, u32[]{:S(2)}) copy-start(bf16[1280,64]{0,1:T(8,128)(2,1)} %param.13) | copy-start | bytes 491524
  13.6 0.7 %copy-start.2 = (bf16[8,32,192]{2,1,0:T(8,128)(2,1)}, bf16[8,32,192]{2,1,0:T(8,128)(2,1)S(1)}, u32[]{:S(2)}) copy-start(bf16[8,32,192]{2,1,0:T(8,128)(2,1)S(1)} %convolution_convert_fusion) | copy-start | bytes 294916
  14.4 0.8 %copy-start.4 = (bf16[8,32,1,128]{3,1,2,0:T(8,128)(2,1)S(1)}, bf16[8,32,1,128]{3,1,2,0:T(8,128)(2,1)}, u32[]{:S(2)}) copy-start(bf16[8,32,1,128]{3,1,2,0:T(8,128)(2,1)} %param.15) | copy-start | bytes 196612
  15.2 14.2 %slice-start = ((bf16[8,32,192]{2,1,0:T(8,128)(2,1)}), bf16[8,32,64]{2,1,0:T(8,128)(2,1)S(1)}, s32[]{:S(2)}) async-start(bf16[8,32,192]{2,1,0:T(8,128)(2,1)} %copy-done.2), calls=%async_computation | async-start | bytes 131072 | tf_op jit(solution)/shard_map/slice | solution.py:46
  45.1 1.5 %collective-permute-start = (bf16[8,8,1,64]{3,1,0,2:T(8,128)(2,1)S(1)}, bf16[8,8,1,64]{3,1,0,2:T(8,128)(2,1)S(1)}, u32[]{:S(2)}, u32[]{:S(2)}) collective-permute-start(bf16[8,8,1,64]{3,1,0,2:T(8,128)(2,1)S(1)} %get-tuple-element.114), channel_id=1, source_target_pairs={{0,3},{1,0},{2,1},{3,2},{4,7},{5,4},{6,5},{7,6},{8,11},{9,8},{10,9... | collective-permute-start | bytes 24584 | tf_op jit(solution)/shard_map/ppermute | solution.py:78
  45.2 3.8 %collective-permute-start.1 = (bf16[8,8,1,64]{3,1,0,2:T(8,128)(2,1)S(1)}, bf16[8,8,1,64]{3,1,0,2:T(8,128)(2,1)S(1)}, u32[]{:S(2)}, u32[]{:S(2)}) collective-permute-start(bf16[8,8,1,64]{3,1,0,2:T(8,128)(2,1)S(1)} %get-tuple-element.113), channel_id=1, source_target_pairs={{0,2},{1,3},{2,0},{3,1},{4,6},{5,7},{6,4},{7,5},{8,10},{9,11},{10,... | collective-permute-start | bytes 24584 | tf_op jit(solution)/shard_map/ppermute | solution.py:78
  46.3 3.2 %collective-permute-start.2 = (bf16[8,8,1,64]{3,1,0,2:T(8,128)(2,1)S(1)}, bf16[8,8,1,64]{3,1,0,2:T(8,128)(2,1)S(1)}, u32[]{:S(2)}, u32[]{:S(2)}) collective-permute-start(bf16[8,8,1,64]{3,1,0,2:T(8,128)(2,1)S(1)} %get-tuple-element.112), channel_id=1, source_target_pairs={{0,1},{1,2},{2,3},{3,0},{4,5},{5,6},{6,7},{7,4},{8,9},{9,10},{10,1... | collective-permute-start | bytes 24584 | tf_op jit(solution)/shard_map/ppermute | solution.py:78
  49.6 0.7 %copy-start.5 = (f32[1280]{0:T(1024)S(1)}, f32[1280]{0:T(1024)}, u32[]{:S(2)}) copy-start(f32[1280]{0:T(1024)} %param.17) | copy-start | bytes 15364
